TPU v7x, 256 devices: a whole 4x4x8 slice. The times are simulated.
256 devices in a mesh: seq: 32 (over y, x, core), exp: 8 (over z).
Axes of the slice: x: 4, y: 4, z: 8, core: 2. Of those that a mesh axis runs over, the one named last changes fastest.
Arguments:
- mixer_input: bfloat16 [4096, 8192], P('seq', 'exp'), may hold values from -6 to 6
- gate_input: bfloat16 [4096, 8192], P('seq', 'exp'), may hold values from -6 to 6
- delta_raw: bfloat16 [4096, 8192], P('seq', 'exp'), may hold values from -7 to 16387
- input_coef: bfloat16 [4096, 16], P('seq'), may hold values from 0.19921875 to 1.796875
- output_coef: bfloat16 [4096, 16], P('seq'), may hold values from -3 to 3
- decay_rate: float32 [16, 8192], P(None, 'exp'), may hold values from 4.8828125e-06 to 0.05
- conv_weight: float32 [4, 8192], P(None, 'exp'), may hold values from -3 to 3
- conv_bias: float32 [8192], P('exp'), may hold values from -3 to 3
- skip_gain: float32 [8192], P('exp'), may hold values from 0.5 to 1.5
- out_weight: bfloat16 [8192, 4096], P('exp', 'seq'), may hold values from -0.0625 to 0.0625
- residual: bfloat16 [4096, 4096], P(('seq', 'exp')), may hold values from -6 to 6
- norm_gain: float32 [4096], replicated, may hold values from 0.1 to 1.9
- router_weight: bfloat16 [4096, 8], replicated, may hold values from -0.09375 to 0.09375
- expert_ids: int32 [4096, 2], P(('seq', 'exp')), may hold values from 0 to 7, all different within a row; in each aligned block of 16 rows (0 to 15, 16 to 31, ...) at most 5 rows name the same one
- gate_weight: bfloat16 [8, 4096, 12288], P('exp', None, 'seq'), may hold values from -0.09375 to 0.09375
- up_weight: bfloat16 [8, 4096, 12288], P('exp', None, 'seq'), may hold values from -0.09375 to 0.09375
- down_weight: bfloat16 [8, 12288, 4096], P('exp', 'seq'), may hold values from -0.0546875 to 0.0546875
Outputs:
- mixed: bfloat16 [4096, 8192], P('seq', 'exp')
- final: bfloat16 [4096, 4096], P(('seq', 'exp'))
Inputs may be any that keep to these rules, and one draw needn't show every extreme that they name: `expert_ids`: each row names two different experts. In each aligned block of 16 rows (the rows of one device) no expert is named by more than 5 rows, and in some block one expert is named by exactly 5 rows.
All inputs are finite; a program needn't handle non-finite values.
Results may differ from a plain program's by a relative error of at most 0.015.
Values may be sent and summed in bfloat16 or wider, within the bound.
No kernel may reach another device: no remote copies, remote signals or barrier semaphores. Data moves between devices by JAX's collectives and lax.ppermute only.
A program may use at most 128 MiB of HBM per device.

v0:
```python
import jax
import jax.numpy as jnp
from jax import lax
from jax.sharding import PartitionSpec as P

KCONV = 4


def from_behind(block, axis, distance):
    devices = range(lax.axis_size(axis))
    route = [(i - distance, i) for i in devices if i - distance in devices]
    return lax.ppermute(block, axis, route)


def carried_in(part, axis, combine, identity):
    place = lax.axis_index(axis)
    gathered = jax.tree.map(lambda a: lax.all_gather(a, axis), part)
    state = jax.tree.map(lambda a, e: jnp.zeros_like(a) + jnp.asarray(e, a.dtype), part, identity)

    def one(turn, state):
        return combine(
            state, jax.tree.map(lambda a: lax.dynamic_index_in_dim(a, turn, 0, False), gathered)
        )

    return lax.fori_loop(0, place, one, state)


def sweep(state, delta, convolved, input_rows, output_rows, decay_rate):

    def advance(carry, inputs):
        delta_row, value_row, input_row, output_row = inputs
        retain = jnp.exp(-delta_row[None, :] * decay_rate)
        carry = retain * carry + (1.0 - retain) * input_row[:, None] * value_row[None, :]
        return (carry, jnp.sum(output_row[:, None] * carry, axis=0))

    return lax.scan(advance, state, (delta, convolved, input_rows, output_rows), unroll=8)


def chain(earlier, later):
    return (earlier[0] * later[0], later[0] * earlier[1] + later[1])


def shards(
    mixer_input,
    gate_input,
    delta_raw,
    input_coef,
    output_coef,
    decay_rate,
    conv_weight,
    conv_bias,
    skip_gain,
    out_weight,
    residual,
    norm_gain,
    router_weight,
    expert_ids,
    gate_weight,
    up_weight,
    down_weight,
):
    length = mixer_input.shape[0]
    width = mixer_input.shape[1]
    tail = mixer_input[length - (KCONV - 1) :]
    before = from_behind(tail, "seq", 1)
    padded = jnp.concatenate([before, mixer_input], axis=0).astype(jnp.float32)
    summed = jnp.broadcast_to(conv_bias[None, :], (length, width))
    for offset in range(KCONV):
        summed = summed + conv_weight[offset][None, :] * padded[offset : offset + length]
    convolved = jax.nn.silu(summed)
    delta = jax.nn.softplus(delta_raw.astype(jnp.float32))
    input_rows = input_coef.astype(jnp.float32)
    output_rows = output_coef.astype(jnp.float32)
    zero_state = jnp.zeros(decay_rate.shape, jnp.float32)
    end_state, local_out = sweep(zero_state, delta, convolved, input_rows, output_rows, decay_rate)
    block_decay = jnp.exp(-jnp.sum(delta, axis=0)[None, :] * decay_rate)
    carried_decay, start_state = carried_in(
        (block_decay, end_state), "seq", chain, (jnp.ones_like(block_decay), zero_state)
    )
    last_state, scan_out = sweep(start_state, delta, convolved, input_rows, output_rows, decay_rate)
    mixed = (
        (scan_out + skip_gain[None, :] * convolved) * jax.nn.silu(gate_input.astype(jnp.float32))
    ).astype(jnp.bfloat16)
    rows = residual.shape[0]
    model_width = residual.shape[1]
    full_weight = lax.all_gather(out_weight, "seq", axis=1, tiled=True)
    projected = lax.psum_scatter(
        jnp.dot(mixed, full_weight, preferred_element_type=jnp.float32).astype(jnp.bfloat16),
        "exp",
        scatter_dimension=0,
        tiled=True,
    ).astype(jnp.float32)
    hidden_state = residual.astype(jnp.float32) + projected
    scale = lax.rsqrt(jnp.mean(hidden_state * hidden_state, axis=1, keepdims=True) + 1e-06)
    normed = (hidden_state * scale * norm_gain[None, :]).astype(jnp.bfloat16)
    experts = router_weight.shape[1]
    capacity = 2 * rows // experts + 1
    logits = jnp.dot(normed, router_weight, preferred_element_type=jnp.float32)
    expert_range = jnp.arange(experts, dtype=jnp.int32)
    matches = expert_ids[:, :, None] == expert_range[None, None, :]
    chosen = jnp.sum(jnp.where(matches, logits[:, None, :], 0.0), axis=2)
    first = jax.nn.sigmoid(chosen[:, 0] - chosen[:, 1])
    flat_ids = expert_ids.reshape(-1)
    onehot = (flat_ids[:, None] == expert_range[None, :]).astype(jnp.int32)
    rank = jnp.sum((jnp.cumsum(onehot, axis=0) - onehot) * onehot, axis=1)
    target = flat_ids * capacity + rank
    placing = (jnp.arange(experts * capacity, dtype=jnp.int32)[:, None] == target[None, :]).astype(
        jnp.bfloat16
    )
    repeated = jnp.broadcast_to(normed[:, None, :], (rows, 2, model_width)).reshape(-1, model_width)
    outgoing = (
        jnp.dot(placing, repeated, preferred_element_type=jnp.float32)
        .astype(jnp.bfloat16)
        .reshape(experts, capacity, model_width)
    )
    arrived = lax.all_to_all(outgoing, "exp", split_axis=0, concat_axis=0, tiled=True)
    flat_rows = arrived.reshape(-1, arrived.shape[2])
    piece = lax.all_gather(flat_rows, "seq", axis=0, tiled=True)
    gating = jnp.dot(piece, gate_weight[0], preferred_element_type=jnp.float32)
    upward = jnp.dot(piece, up_weight[0], preferred_element_type=jnp.float32)
    activated = (jax.nn.silu(gating) * upward).astype(jnp.bfloat16)
    partial_out = jnp.dot(activated, down_weight[0], preferred_element_type=jnp.float32)
    summed_out = lax.psum_scatter(
        partial_out.astype(jnp.bfloat16), "seq", scatter_dimension=0, tiled=True
    )
    returned = lax.all_to_all(
        summed_out.reshape(arrived.shape), "exp", split_axis=0, concat_axis=0, tiled=True
    )
    flat_returned = returned.reshape(-1, model_width)
    picked = jnp.einsum(
        "sa,sd->ad", placing, flat_returned, preferred_element_type=jnp.float32
    ).reshape(rows, 2, model_width)
    moe_out = first[:, None] * picked[:, 0] + (1.0 - first)[:, None] * picked[:, 1]
    final = (hidden_state + moe_out).astype(jnp.bfloat16)
    return (mixed, final)


def solution(mesh):
    return jax.shard_map(
        shards,
        mesh=mesh,
        in_specs=(
            P("seq", "exp"),
            P("seq", "exp"),
            P("seq", "exp"),
            P("seq", None),
            P("seq", None),
            P(None, "exp"),
            P(None, "exp"),
            P("exp"),
            P("exp"),
            P("exp", "seq"),
            P(("seq", "exp"), None),
            P(),
            P(),
            P(("seq", "exp"), None),
            P("exp", None, "seq"),
            P("exp", None, "seq"),
            P("exp", "seq", None),
        ),
        out_specs=(P("seq", "exp"), P(("seq", "exp"), None)),
        check_vma=False,
    )
```

profile of v0, /device:TPU:2, one launch (start us, length us, event | category | flops | bytes accessed | tf_op | source)
XLA Modules:
  0.0 490.1 jit_solution(7569274445757107317)
XLA Ops:
  8.1 2.0 collective-permute-start
  10.2 2.1 fusion.59
  17.4 1.8 fusion.81
  19.2 28.9 %while.37 = (s32[]{:T(128)}, f32[16,1024]{1,0:T(8,128)S(1)}, f32[16,8,1024]{2,1,0:T(8,128)}, f32[16,1024]{1,0:T(8,128)S(1)}, f32[16,8,16]{2,1,0:T(8,128)S(1)}, /...) while((s32[]{:T(128)}, f32[16,1024]{1,0:T(8,128)S(1)}, ...), condition=%wide.region_2.3_spmd.clone, body=%wide.region_1.2_spmd.clone.sunk | while | flops 811018 | bytes 396055 | solution.py:36
  20.8 1.6 constant_dynamic-slice_fusion.41
  22.6 1.6 constant_dynamic-slice_fusion.41
  26.1 1.6 constant_dynamic-slice_fusion.41
  27.9 1.9 constant_dynamic-slice_fusion.41
  30.0 1.6 constant_dynamic-slice_fusion.41
  31.9 1.5 constant_dynamic-slice_fusion.41
  35.3 1.5 constant_dynamic-slice_fusion.41
  37.0 1.9 constant_dynamic-slice_fusion.41
  39.1 1.6 constant_dynamic-slice_fusion.41
  40.9 1.6 constant_dynamic-slice_fusion.41
  42.8 1.6 constant_dynamic-slice_fusion.41
  44.6 1.6 constant_dynamic-slice_fusion.41
  46.4 1.6 constant_dynamic-slice_fusion.41
  49.7 16.5 %all-gather.11.cloned.1.call-done = f32[512,1024]{1,0:T(8,128)} async-done(((f32[16,1024]{1,0:T(8,128)}), f32[512,1024]{1,0:T(8,128)}) %all-gather.11.cloned.1.call-update) | async-done | bytes 2097168 | tf_op jit(solution)/shard_map/all_gather | solution.py:17
  66.2 51.3 %all-gather.13.cloned.1.call-done = f32[512,1024]{1,0:T(8,128)} async-done(((f32[16,1024]{1,0:T(8,128)}), f32[512,1024]{1,0:T(8,128)}) %all-gather.13.cloned.1.call-update) | async-done | bytes 2097168 | tf_op jit(solution)/shard_map/all_gather | solution.py:17
  117.5 1.8 while.35
  119.4 44.5 %while.36 = (s32[]{:T(128)}, f32[16,1024]{1,0:T(8,128)S(1)}, f32[16,8,1024]{2,1,0:T(8,128)}, f32[16,8,1024]{2,1,0:T(8,128)}, f32[16,1024]{1,0:T(8,128)S(1)}, /*i...) while((s32[]{:T(128)}, f32[16,1024]{1,0:T(8,128)S(1)}, ...), condition=%wide.region_14.15_spmd, body=%wide.region_5.14_spmd.sunk | while | flops 1441801 | bytes 1316385 | solution.py:36
  122.0 1.6 constant_dynamic-slice_fusion.40
  124.8 1.6 constant_dynamic-slice_fusion.40
  130.2 1.6 constant_dynamic-slice_fusion.40
  133.0 1.9 constant_dynamic-slice_fusion.40
  136.1 1.6 constant_dynamic-slice_fusion.40
  138.9 1.5 constant_dynamic-slice_fusion.40
  144.2 1.5 constant_dynamic-slice_fusion.40
  146.9 1.9 constant_dynamic-slice_fusion.40
  150.0 1.6 constant_dynamic-slice_fusion.40
  152.8 1.6 constant_dynamic-slice_fusion.40
  155.6 1.6 constant_dynamic-slice_fusion.40
  158.3 1.6 constant_dynamic-slice_fusion.40
  161.1 1.6 constant_dynamic-slice_fusion.40
  163.8 2.5 fusion.58
  166.4 17.6 %all-gather.7.cloned.1.call-done = bf16[1024,4096]{1,0:T(8,128)(2,1)} async-done(((bf16[1024,128]{1,0:T(8,128)(2,1)}), bf16[1024,4096]{1,0:T(8,128)(2,1)}) %all-gather.7.cloned.1.call-update) | async-done | bytes 8388624 | tf_op jit(solution)/shard_map/all_gather | solution.py:86
  184.0 5.7 %convolution_convert_fusion.1 = bf16[128,4096]{1,0:T(8,128)(2,1)} fusion(bf16[128,1024]{1,0:T(8,128)(2,1)S(1)} %fusion.58, bf16[1024,4096]{1,0:T(8,128)(2,1)} %all-gather.7.cloned.1.call-done), kind=kOutput, calls=%fused_computation.111 | convolution fusion | flops 1074266112 | bytes 9699328 | tf_op jit(solution)/shard_map/dot_general | solution.py:88
  191.5 45.4 %reduce-scatter.3.cloned.1.call-done = bf16[16,4096]{1,0:T(8,128)(2,1)} async-done(((bf16[128,4096]{1,0:T(8,128)(2,1)}), bf16[16,4096]{1,0:T(8,128)(2,1)}) %reduce-scatter.3.cloned.1.call-update) | async-done | bytes 131088 | tf_op jit(solution)/shard_map/reduce_scatter | solution.py:87
  242.8 17.9 %all_to_all.10 = bf16[8,5,4096]{2,1,0:T(8,128)(2,1)} all-to-all(bf16[8,5,4096]{2,1,0:T(8,128)(2,1)} %reshape.356), channel_id=1, replica_groups=mesh['seq'=32,'exp'=8] {'exp'}, dimensions={0} | all-to-all | bytes 655360 | tf_op jit(solution)/shard_map/all_to_all | solution.py:116
  260.7 1.9 reshape.357
  262.6 59.5 %all-gather.9.cloned.1.call-done = bf16[1280,4096]{1,0:T(8,128)(2,1)} async-done(((bf16[40,4096]{1,0:T(8,128)(2,1)}), bf16[1280,4096]{1,0:T(8,128)(2,1)}) %all-gather.9.cloned.1.call-update) | async-done | bytes 10485776 | tf_op jit(solution)/shard_map/all_gather | solution.py:118
  322.2 10.2 %fusion.33 = f32[1280,384]{1,0:T(8,128)} fusion(bf16[1280,4096]{1,0:T(8,128)(2,1)} %all-gather.9.cloned.1.call-done, bf16[1,4096,384]{2,1,0:T(8,128)(2,1)} %param.37), kind=kOutput, calls=%fused_computation.116 | convolution fusion | flops 4026531840 | bytes 15597568 | tf_op jit(solution)/shard_map/dot_general | solution.py:119
  332.3 17.2 %convolution_convert_fusion = bf16[1280,4096]{1,0:T(8,128)(2,1)} fusion(bf16[1,384,4096]{2,1,0:T(8,128)(2,1)S(1)} %copy-done, bf16[1280,4096]{1,0:T(8,128)(2,1)} %all-gather.9.cloned.1.call-done, bf16[1,4096,384]{2,1,0:T(8,128)(2,1)} %param.38, f32[1280,384]{1,0:T(8,128)} %fusion.33), kind=kOutput, calls=%fused_computation.110 | convolution fusion | flops 8061255680 | bytes 29229056 | tf_op jit(solution)/shard_map/dot_general | solution.py:122
  349.6 105.2 %reduce-scatter.5.cloned.1.call-done = bf16[40,4096]{1,0:T(8,128)(2,1)} async-done(((bf16[1280,4096]{1,0:T(8,128)(2,1)}), bf16[40,4096]{1,0:T(8,128)(2,1)}) %reduce-scatter.5.cloned.1.call-update) | async-done | bytes 327696 | tf_op jit(solution)/shard_map/reduce_scatter | solution.py:123
  454.8 1.9 reshape.358
  456.7 7.0 %all-to-all-start.1 = ((bf16[8,5,4096]{2,1,0:T(8,128)(2,1)}), bf16[8,5,4096]{2,1,0:T(8,128)(2,1)}, u32[]{:S(2)}, u32[]{:S(2)}) async-start(bf16[8,5,4096]{2,1,0:T(8,128)(2,1)} %reshape.358), calls=%async_computation.3 | async-start | bytes 1048576 | tf_op jit(solution)/shard_map/all_to_all | solution.py:126
  464.0 16.1 %all-to-all-done.1 = bf16[8,5,4096]{2,1,0:T(8,128)(2,1)} async-done(((bf16[8,5,4096]{2,1,0:T(8,128)(2,1)}), bf16[8,5,4096]{2,1,0:T(8,128)(2,1)}, u32[]{:S(2)}, u32[]{:S(2)}) %all-to-all-start.1) | async-done | bytes 327712 | tf_op jit(solution)/shard_map/all_to_all | solution.py:126
  481.6 1.7 fusion.64
  (273 shorter events, 48.7 us)
Async XLA Ops:
  7.2 325.2 %copy-start = (bf16[1,384,4096]{2,1,0:T(8,128)(2,1)S(1)}, bf16[1,384,4096]{2,1,0:T(8,128)(2,1)}, u32[]{:S(2)}) copy-start(bf16[1,384,4096]{2,1,0:T(8,128)(2,1)} %param.39) | copy-start | bytes 9437188
  7.2 12.0 %copy-start.2 = (f32[16,1024]{1,0:T(8,128)S(1)}, f32[16,1024]{1,0:T(8,128)}, u32[]{:S(2)}) copy-start(f32[16,1024]{1,0:T(8,128)} %param.28) | copy-start | bytes 196612
  7.2 59.0 %all-gather.11.cloned.1.call-start = ((), (), s32[]{:S(2)}) async-start(), calls=%async_computation.8 | async-start | bytes 2162688 | tf_op jit(solution)/shard_map/all_gather | solution.py:17
  8.1 7.4 %collective-permute-start = (bf16[3,1024]{1,0:T(4,128)(2,1)S(1)}, bf16[3,1024]{1,0:T(4,128)(2,1)S(1)}, u32[]{:S(2)}, u32[]{:S(2)}) collective-permute-start(bf16[3,1024]{1,0:T(4,128)(2,1)S(1)} %slice.264), channel_id=1, source_target_pairs={{0,8},{8,16},{16,24},{24,32},{32,40},{40,48},{48,56},{56,64},{64,7... | collective-permute-start | bytes 18440 | tf_op jit(solution)/shard_map/ppermute | solution.py:12
  13.8 103.8 %all-gather.13.cloned.1.call-start = ((), (), s32[]{:S(2)}) async-start(), calls=%async_computation.9 | async-start | bytes 2162688 | tf_op jit(solution)/shard_map/all_gather | solution.py:17
  16.5 0.8 copy-start.1
  16.5 33.1 %copy-start.12 = (bf16[128,16]{0,1:T(8,128)(2,1)S(1)}, bf16[128,16]{0,1:T(8,128)(2,1)}, u32[]{:S(2)}) copy-start(bf16[128,16]{0,1:T(8,128)(2,1)} %param.27) | copy-start | bytes 12292
  48.1 0.6 copy-start.3
  48.8 135.2 %all-gather.7.cloned.1.call-start = ((), (), s32[]{:S(2)}) async-start(), calls=%async_computation.4 | async-start | bytes 8650752 | tf_op jit(solution)/shard_map/all_gather | solution.py:86
  49.5 187.4 %reduce-scatter.3.cloned.1.call-start = ((), (), s32[]{:S(2)}) async-start(), calls=%async_computation.5 | async-start | bytes 1179648 | tf_op jit(solution)/shard_map/reduce_scatter | solution.py:87
  119.3 44.5 %copy-start.9 = (f32[1024]{0:T(1024)S(1)}, f32[1024]{0:T(1024)}, u32[]{:S(2)}) copy-start(f32[1024]{0:T(1024)} %param.30) | copy-start | bytes 12292
  119.4 44.5 %copy-start.11 = (f32[1024]{0:T(1024)S(1)}, f32[1024]{0:T(1024)}, u32[]{:S(2)}) copy-start(f32[1024]{0:T(1024)} %param.31) | copy-start | bytes 12292
  166.3 23.4 %copy-start.4 = (bf16[128,1024]{1,0:T(8,128)(2,1)}, bf16[128,1024]{1,0:T(8,128)(2,1)S(1)}, u32[]{:S(2)}) copy-start(bf16[128,1024]{1,0:T(8,128)(2,1)S(1)} %fusion.58) | copy-start | bytes 786436
  166.4 70.6 %copy-start.7 = (bf16[16,4096]{1,0:T(8,128)(2,1)S(1)}, bf16[16,4096]{1,0:T(8,128)(2,1)}, u32[]{:S(2)}) copy-start(bf16[16,4096]{1,0:T(8,128)(2,1)} %param.33) | copy-start | bytes 393220
  166.4 71.6 %copy-start.10 = (f32[4096]{0:T(1024)S(1)}, f32[4096]{0:T(1024)}, u32[]{:S(2)}) copy-start(f32[4096]{0:T(1024)} %param.34) | copy-start | bytes 49156
  189.7 132.4 %all-gather.9.cloned.1.call-start = ((), (), s32[]{:S(2)}) async-start(), calls=%async_computation.6 | async-start | bytes 10813440 | tf_op jit(solution)/shard_map/all_gather | solution.py:118
  239.0 0.7 copy-start.5
  262.6 192.2 %reduce-scatter.5.cloned.1.call-start = ((), (), s32[]{:S(2)}) async-start(), calls=%async_computation.7 | async-start | bytes 10813440 | tf_op jit(solution)/shard_map/reduce_scatter | solution.py:123
  349.6 114.2 %copy-start.14 = (s32[32]{0:T(128)S(1)}, s32[32]{0:T(128)}, u32[]{:S(2)}) copy-start(s32[32]{0:T(128)} %multiply_add_fusion.8) | copy-start | bytes 388
  349.6 114.3 %copy-start.6 = (bf16[16,4096]{1,0:T(8,128)(2,1)S(1)}, bf16[16,4096]{1,0:T(8,128)(2,1)}, u32[]{:S(2)}) copy-start(bf16[16,4096]{1,0:T(8,128)(2,1)} %copy-done.5) | copy-start | bytes 393220
  349.6 114.3 %copy-start.8 = (bf16[4096,8]{0,1:T(8,128)(2,1)S(1)}, bf16[4096,8]{0,1:T(8,128)(2,1)}, u32[]{:S(2)}) copy-start(bf16[4096,8]{0,1:T(8,128)(2,1)} %param.35) | copy-start | bytes 196612
  349.6 114.4 %copy-start.13 = (s32[16,2]{0,1:T(2,128)S(1)}, s32[16,2]{0,1:T(2,128)}, u32[]{:S(2)}) copy-start(s32[16,2]{0,1:T(2,128)} %param.36) | copy-start | bytes 388
  456.7 23.4 %all-to-all-start.1 = ((bf16[8,5,4096]{2,1,0:T(8,128)(2,1)}), bf16[8,5,4096]{2,1,0:T(8,128)(2,1)}, u32[]{:S(2)}, u32[]{:S(2)}) async-start(bf16[8,5,4096]{2,1,0:T(8,128)(2,1)} %reshape.358), calls=%async_computation.3 | async-start | bytes 1048576 | tf_op jit(solution)/shard_map/all_to_all | solution.py:126
Sparse Core Ops, SparseCore 0:
  13.9 52.2 all-gather.10
  69.3 48.1 all-gather.12
  120.0 63.9 all-gather.6
  189.9 47.0 reduce-scatter.2
  262.7 59.3 all-gather.8
  349.7 105.0 reduce-scatter.4
where the time goes:
time: 497 us; the launch traced here: 490 us
  waiting for transfers between devices  312 us (63%)
  other arithmetic  76.2 us (15%)
  matrix products  34.6 us (7%)
  local copies, waits for them, and re-layouts  24.2 us (5%)
  blocking collectives  17.9 us (4%)
  between operations  14.4 us (3%)
  starting transfers between devices  9.3 us (2%)
    reduce_scatter x1, waiting for transfers between devices, shards(): lax.psum_scatter(partial_out.astype(jnp.bfloat16), 'seq', scatter_dimensi...  105 us
    all_gather x2, waiting for transfers between devices, carried_in(): gathered = jax.tree.map(lambda a: lax.all_gather(a, axis), part)  67.8 us
    all_gather x1, waiting for transfers between devices, shards(): piece = lax.all_gather(flat_rows, 'seq', axis=0, tiled=True)  59.5 us
    slice x32, other arithmetic, sweep(): lax.scan(advance, state, (delta, convolved, input_rows, output_rows), unr...  50.8 us
    reduce_scatter x1, waiting for transfers between devices, shards(): lax.psum_scatter(jnp.dot(mixed, full_weight, preferred_element_type=jnp.f...  45.4 us
    all_to_all x1, blocking collectives, shards(): lax.all_to_all(outgoing, 'exp', split_axis=0, concat_axis=0, tiled=True)  17.9 us
    all_gather x1, waiting for transfers between devices, shards(): full_weight = lax.all_gather(out_weight, 'seq', axis=1, tiled=True)  17.6 us
    dot_general x1, matrix products, shards(): jnp.dot(activated, down_weight[0], preferred_element_type=jnp.float32)  17.2 us
  transfers between devices with their start and end apart: 8, of which 7 were waited for; matrix products, arithmetic and copies ran while one was open for 18% of the time, Pallas kernels for 0%

commit v1 on v0

--- a/solution.py
+++ b/solution.py
@@ -115,7 +115,9 @@
     )
     arrived = lax.all_to_all(outgoing, "exp", split_axis=0, concat_axis=0, tiled=True)
     flat_rows = arrived.reshape(-1, arrived.shape[2])
-    piece = lax.all_gather(flat_rows, "seq", axis=0, tiled=True)
+    piece = jnp.concatenate(
+        lax.all_to_all(jnp.stack([flat_rows] * lax.axis_size("seq")), "seq", 0, 0), axis=0
+    )
     gating = jnp.dot(piece, gate_weight[0], preferred_element_type=jnp.float32)
     upward = jnp.dot(piece, up_weight[0], preferred_element_type=jnp.float32)
     activated = (jax.nn.silu(gating) * upward).astype(jnp.bfloat16)

time: 497 us -> 559 us (1.12)
  blocking collectives: 17.9 us -> 143 us
  waiting for transfers between devices: 312 us -> 254 us
  other arithmetic: 76.2 us -> 68.1 us
  local copies, waits for them, and re-layouts: 24.2 us -> 31.7 us
    all_to_all x0 -> x1, blocking collectives: none -> 125 us  [shards(): lax.all_to_all(jnp.stack([flat_rows] * lax.axis_size('seq')), 'seq', 0, 0)]
    all_gather x1 -> x0, waiting for transfers between devices: 59.5 us -> none  [shards(): piece = lax.all_gather(flat_rows, 'seq', axis=0, tiled=True)]
    slice x32, other arithmetic: 50.8 us -> 43.1 us  [sweep(): lax.scan(advance, state, (delta, convolved, input_rows, output_rows), unr...]
    another operation x0 -> x2, local copies, waits for them, and re-layouts: none -> 6.47 us  [shards(): jnp.stack([flat_rows] * lax.axis_size('seq'))]
  transfers between devices with their start and end apart: 8 -> 7, of which waited for: 7 -> 6; matrix products, arithmetic and copies ran while one was open for 18% -> 14% of each run, Pallas kernels for 0% -> 0%
where the time goes in v1:
time: 559 us; the launch traced here: 553 us
  waiting for transfers between devices  254 us (45%)
  blocking collectives  143 us (26%)
  other arithmetic  68.1 us (12%)
  local copies, waits for them, and re-layouts  31.7 us (6%)
  matrix products  31.4 us (6%)
  between operations  14 us (3%)
  starting transfers between devices  9.25 us (2%)
    all_to_all x1, blocking collectives, shards(): lax.all_to_all(jnp.stack([flat_rows] * lax.axis_size('seq')), 'seq', 0, 0)  125 us
    reduce_scatter x1, waiting for transfers between devices, shards(): lax.psum_scatter(partial_out.astype(jnp.bfloat16), 'seq', scatter_dimensi...  101 us
    all_gather x2, waiting for transfers between devices, carried_in(): gathered = jax.tree.map(lambda a: lax.all_gather(a, axis), part)  71.7 us
    slice x32, other arithmetic, sweep(): lax.scan(advance, state, (delta, convolved, input_rows, output_rows), unr...  43.1 us
    reduce_scatter x1, waiting for transfers between devices, shards(): lax.psum_scatter(jnp.dot(mixed, full_weight, preferred_element_type=jnp.f...  42.5 us
    all_gather x1, waiting for transfers between devices, shards(): full_weight = lax.all_gather(out_weight, 'seq', axis=1, tiled=True)  21.6 us
    all_to_all x1, blocking collectives, shards(): lax.all_to_all(outgoing, 'exp', split_axis=0, concat_axis=0, tiled=True)  17.9 us
    dot_general x1, matrix products, shards(): jnp.dot(activated, down_weight[0], preferred_element_type=jnp.float32)  17.3 us
  transfers between devices with their start and end apart: 7, of which 6 were waited for; matrix products, arithmetic and copies ran while one was open for 14% of the time, Pallas kernels for 0%

profile of v1, /device:TPU:2, one launch (start us, length us, event | category | flops | bytes accessed | tf_op | source)
XLA Modules:
  0.0 552.7 jit_solution(16250137498817357403)
XLA Ops:
  8.1 2.0 collective-permute-start
  10.2 2.1 fusion.59
  12.2 1.5 multiply_exponential_fusion
  17.4 1.8 fusion.81
  19.2 25.1 %while.37 = (s32[]{:T(128)}, f32[16,1024]{1,0:T(8,128)S(1)}, f32[16,8,1024]{2,1,0:T(8,128)}, f32[16,1024]{1,0:T(8,128)S(1)}, f32[16,8,16]{2,1,0:T(8,128)S(1)}, /...) while((s32[]{:T(128)}, f32[16,1024]{1,0:T(8,128)S(1)}, ...), condition=%wide.region_2.3_spmd.clone, body=%wide.region_1.2_spmd.clone.sunk | while | flops 811018 | bytes 396055 | solution.py:36
  20.7 1.6 constant_dynamic-slice_fusion.41
  22.5 1.3 constant_dynamic-slice_fusion.41
  24.0 1.3 constant_dynamic-slice_fusion.41
  27.1 1.4 constant_dynamic-slice_fusion.41
  33.3 1.3 constant_dynamic-slice_fusion.41
  34.8 1.5 constant_dynamic-slice_fusion.41
  36.6 1.3 constant_dynamic-slice_fusion.41
  38.1 1.3 constant_dynamic-slice_fusion.41
  39.7 1.3 constant_dynamic-slice_fusion.41
  41.2 1.3 constant_dynamic-slice_fusion.41
  42.8 1.3 constant_dynamic-slice_fusion.41
  45.8 20.4 %all-gather.8.cloned.1.call-done = f32[512,1024]{1,0:T(8,128)} async-done(((f32[16,1024]{1,0:T(8,128)}), f32[512,1024]{1,0:T(8,128)}) %all-gather.8.cloned.1.call-update) | async-done | bytes 2097168 | tf_op jit(solution)/shard_map/all_gather | solution.py:17
  66.2 51.3 %all-gather.10.cloned.1.call-done = f32[512,1024]{1,0:T(8,128)} async-done(((f32[16,1024]{1,0:T(8,128)}), f32[512,1024]{1,0:T(8,128)}) %all-gather.10.cloned.1.call-update) | async-done | bytes 2097168 | tf_op jit(solution)/shard_map/all_gather | solution.py:17
  117.5 1.8 while.35
  119.4 40.5 %while.36 = (s32[]{:T(128)}, f32[16,1024]{1,0:T(8,128)S(1)}, f32[16,8,1024]{2,1,0:T(8,128)}, f32[16,8,1024]{2,1,0:T(8,128)}, f32[16,1024]{1,0:T(8,128)S(1)}, /*i...) while((s32[]{:T(128)}, f32[16,1024]{1,0:T(8,128)S(1)}, ...), condition=%wide.region_14.15_spmd, body=%wide.region_5.14_spmd.sunk | while | flops 1441801 | bytes 1316385 | solution.py:36
  121.9 1.6 constant_dynamic-slice_fusion.40
  124.7 1.3 constant_dynamic-slice_fusion.40
  127.2 1.3 constant_dynamic-slice_fusion.40
  132.1 1.4 constant_dynamic-slice_fusion.40
  134.7 1.3 constant_dynamic-slice_fusion.40
  139.7 1.3 constant_dynamic-slice_fusion.40
  142.2 1.3 constant_dynamic-slice_fusion.40
  144.7 1.5 constant_dynamic-slice_fusion.40
  147.4 1.3 constant_dynamic-slice_fusion.40
  149.9 1.3 constant_dynamic-slice_fusion.40
  152.4 1.3 constant_dynamic-slice_fusion.40
  154.9 1.3 constant_dynamic-slice_fusion.40
  157.4 1.3 constant_dynamic-slice_fusion.40
  159.9 2.5 fusion.58
  162.4 21.6 %all-gather.6.cloned.1.call-done = bf16[1024,4096]{1,0:T(8,128)(2,1)} async-done(((bf16[1024,128]{1,0:T(8,128)(2,1)}), bf16[1024,4096]{1,0:T(8,128)(2,1)}) %all-gather.6.cloned.1.call-update) | async-done | bytes 8388624 | tf_op jit(solution)/shard_map/all_gather | solution.py:86
  184.0 5.7 %convolution_convert_fusion.1 = bf16[128,4096]{1,0:T(8,128)(2,1)} fusion(bf16[128,1024]{1,0:T(8,128)(2,1)S(1)} %fusion.58, bf16[1024,4096]{1,0:T(8,128)(2,1)} %all-gather.6.cloned.1.call-done), kind=kOutput, calls=%fused_computation.111 | convolution fusion | flops 1074266112 | bytes 9699328 | tf_op jit(solution)/shard_map/dot_general | solution.py:88
  190.3 42.5 %reduce-scatter.3.cloned.1.call-done = bf16[16,4096]{1,0:T(8,128)(2,1)} async-done(((bf16[128,4096]{1,0:T(8,128)(2,1)}), bf16[16,4096]{1,0:T(8,128)(2,1)}) %reduce-scatter.3.cloned.1.call-update) | async-done | bytes 131088 | tf_op jit(solution)/shard_map/reduce_scatter | solution.py:87
  238.8 17.9 %all_to_all.15 = bf16[8,5,4096]{2,1,0:T(8,128)(2,1)} all-to-all(bf16[8,5,4096]{2,1,0:T(8,128)(2,1)} %reshape.358), channel_id=1, replica_groups=mesh['seq'=32,'exp'=8] {'exp'}, dimensions={0} | all-to-all | bytes 655360 | tf_op jit(solution)/shard_map/all_to_all | solution.py:116
  257.9 5.3 stack.3
  263.2 124.9 %all_to_all.16 = bf16[32,40,4096]{2,1,0:T(8,128)(2,1)S(1)} all-to-all(bf16[32,40,4096]{2,1,0:T(8,128)(2,1)} %stack.3), channel_id=1, replica_groups=mesh['seq'=32,'exp'=8] {'seq'}, dimensions={0} | all-to-all | bytes 20971520 | tf_op jit(solution)/shard_map/all_to_all | solution.py:119
  388.1 3.8 copy-done.3
  391.9 6.9 %fusion.33 = f32[1280,384]{1,0:T(8,128)} fusion(bf16[1280,4096]{1,0:T(8,128)(2,1)S(1)} %bitcast.247, bf16[1,4096,384]{2,1,0:T(8,128)(2,1)S(1)} %copy-done.14), kind=kOutput, calls=%fused_computation.116 | convolution fusion | flops 4026531840 | bytes 15597568 | tf_op jit(solution)/shard_map/dot_general | solution.py:121
  398.8 17.3 %convolution_convert_fusion = bf16[1280,4096]{1,0:T(8,128)(2,1)} fusion(bf16[1,384,4096]{2,1,0:T(8,128)(2,1)S(1)} %copy-done, bf16[1280,4096]{1,0:T(8,128)(2,1)} %bitcast.248, bf16[1,4096,384]{2,1,0:T(8,128)(2,1)} %param.38, f32[1280,384]{1,0:T(8,128)} %fusion.33), kind=kOutput, calls=%fused_computation.110 | convolution fusion | flops 8061255680 | bytes 29229056 | tf_op jit(solution)/shard_map/dot_general | solution.py:124
  416.1 101.5 %reduce-scatter.5.cloned.1.call-done = bf16[40,4096]{1,0:T(8,128)(2,1)} async-done(((bf16[1280,4096]{1,0:T(8,128)(2,1)}), bf16[40,4096]{1,0:T(8,128)(2,1)}) %reduce-scatter.5.cloned.1.call-update) | async-done | bytes 327696 | tf_op jit(solution)/shard_map/reduce_scatter | solution.py:125
  517.6 1.9 reshape.360
  519.5 7.0 %all-to-all-start.2 = ((bf16[8,5,4096]{2,1,0:T(8,128)(2,1)}), bf16[8,5,4096]{2,1,0:T(8,128)(2,1)}, u32[]{:S(2)}, u32[]{:S(2)}) async-start(bf16[8,5,4096]{2,1,0:T(8,128)(2,1)} %reshape.360), calls=%async_computation.4 | async-start | bytes 1048576 | tf_op jit(solution)/shard_map/all_to_all | solution.py:128
  526.8 16.2 %all-to-all-done.2 = bf16[8,5,4096]{2,1,0:T(8,128)(2,1)} async-done(((bf16[8,5,4096]{2,1,0:T(8,128)(2,1)}), bf16[8,5,4096]{2,1,0:T(8,128)(2,1)}, u32[]{:S(2)}, u32[]{:S(2)}) %all-to-all-start.2) | async-done | bytes 327712 | tf_op jit(solution)/shard_map/all_to_all | solution.py:128
  544.4 1.7 fusion.64
  (272 shorter events, 49.0 us)
Async XLA Ops:
  7.2 391.7 %copy-start = (bf16[1,384,4096]{2,1,0:T(8,128)(2,1)S(1)}, bf16[1,384,4096]{2,1,0:T(8,128)(2,1)}, u32[]{:S(2)}) copy-start(bf16[1,384,4096]{2,1,0:T(8,128)(2,1)} %param.39) | copy-start | bytes 9437188
  7.2 12.0 %copy-start.2 = (f32[16,1024]{1,0:T(8,128)S(1)}, f32[16,1024]{1,0:T(8,128)}, u32[]{:S(2)}) copy-start(f32[16,1024]{1,0:T(8,128)} %param.28) | copy-start | bytes 196612
  7.2 59.0 %all-gather.8.cloned.1.call-start = ((), (), s32[]{:S(2)}) async-start(), calls=%async_computation.8 | async-start | bytes 2162688 | tf_op jit(solution)/shard_map/all_gather | solution.py:17
  8.1 7.4 %collective-permute-start = (bf16[3,1024]{1,0:T(4,128)(2,1)S(1)}, bf16[3,1024]{1,0:T(4,128)(2,1)S(1)}, u32[]{:S(2)}, u32[]{:S(2)}) collective-permute-start(bf16[3,1024]{1,0:T(4,128)(2,1)S(1)} %slice.264), channel_id=1, source_target_pairs={{0,8},{8,16},{16,24},{24,32},{32,40},{40,48},{48,56},{56,64},{64,7... | collective-permute-start | bytes 18440 | tf_op jit(solution)/shard_map/ppermute | solution.py:12
  13.8 103.8 %all-gather.10.cloned.1.call-start = ((), (), s32[]{:S(2)}) async-start(), calls=%async_computation.9 | async-start | bytes 2162688 | tf_op jit(solution)/shard_map/all_gather | solution.py:17
  16.5 0.8 copy-start.1
  16.5 29.2 %copy-start.12 = (bf16[128,16]{0,1:T(8,128)(2,1)S(1)}, bf16[128,16]{0,1:T(8,128)(2,1)}, u32[]{:S(2)}) copy-start(bf16[128,16]{0,1:T(8,128)(2,1)} %param.27) | copy-start | bytes 12292
  44.3 0.6 copy-start.4
  44.9 139.1 %all-gather.6.cloned.1.call-start = ((), (), s32[]{:S(2)}) async-start(), calls=%async_computation.5 | async-start | bytes 8650752 | tf_op jit(solution)/shard_map/all_gather | solution.py:86
  45.7 187.2 %reduce-scatter.3.cloned.1.call-start = ((), (), s32[]{:S(2)}) async-start(), calls=%async_computation.6 | async-start | bytes 1179648 | tf_op jit(solution)/shard_map/reduce_scatter | solution.py:87
  119.4 40.5 %copy-start.9 = (f32[1024]{0:T(1024)S(1)}, f32[1024]{0:T(1024)}, u32[]{:S(2)}) copy-start(f32[1024]{0:T(1024)} %param.30) | copy-start | bytes 12292
  119.4 40.5 %copy-start.11 = (f32[1024]{0:T(1024)S(1)}, f32[1024]{0:T(1024)}, u32[]{:S(2)}) copy-start(f32[1024]{0:T(1024)} %param.31) | copy-start | bytes 12292
  162.4 27.3 %copy-start.5 = (bf16[128,1024]{1,0:T(8,128)(2,1)}, bf16[128,1024]{1,0:T(8,128)(2,1)S(1)}, u32[]{:S(2)}) copy-start(bf16[128,1024]{1,0:T(8,128)(2,1)S(1)} %fusion.58) | copy-start | bytes 786436
  162.4 27.4 %copy-start.13 = (s32[16,2]{0,1:T(2,128)S(1)}, s32[16,2]{0,1:T(2,128)}, u32[]{:S(2)}) copy-start(s32[16,2]{0,1:T(2,128)} %param.36) | copy-start | bytes 388
  162.4 71.5 %copy-start.10 = (f32[4096]{0:T(1024)S(1)}, f32[4096]{0:T(1024)}, u32[]{:S(2)}) copy-start(f32[4096]{0:T(1024)} %param.34) | copy-start | bytes 49156
  189.7 327.9 %reduce-scatter.5.cloned.1.call-start = ((), (), s32[]{:S(2)}) async-start(), calls=%async_computation.7 | async-start | bytes 10813440 | tf_op jit(solution)/shard_map/reduce_scatter | solution.py:125
  235.0 0.7 copy-start.6
  263.2 128.8 %copy-start.14 = (bf16[1,4096,384]{2,1,0:T(8,128)(2,1)S(1)}, bf16[1,4096,384]{2,1,0:T(8,128)(2,1)}, u32[]{:S(2)}) copy-start(bf16[1,4096,384]{2,1,0:T(8,128)(2,1)} %param.37) | copy-start | bytes 9437188
  388.1 3.8 copy-start.3
  416.1 110.5 %copy-start.7 = (bf16[16,4096]{1,0:T(8,128)(2,1)S(1)}, bf16[16,4096]{1,0:T(8,128)(2,1)}, u32[]{:S(2)}) copy-start(bf16[16,4096]{1,0:T(8,128)(2,1)} %copy-done.6) | copy-start | bytes 393220
  416.1 110.5 %copy-start.8 = (bf16[4096,8]{0,1:T(8,128)(2,1)S(1)}, bf16[4096,8]{0,1:T(8,128)(2,1)}, u32[]{:S(2)}) copy-start(bf16[4096,8]{0,1:T(8,128)(2,1)} %param.35) | copy-start | bytes 196612
  519.5 23.5 %all-to-all-start.2 = ((bf16[8,5,4096]{2,1,0:T(8,128)(2,1)}), bf16[8,5,4096]{2,1,0:T(8,128)(2,1)}, u32[]{:S(2)}, u32[]{:S(2)}) async-start(bf16[8,5,4096]{2,1,0:T(8,128)(2,1)} %reshape.360), calls=%async_computation.4 | async-start | bytes 1048576 | tf_op jit(solution)/shard_map/all_to_all | solution.py:128
Sparse Core Ops, SparseCore 0:
  13.9 52.2 all-gather.7
  69.3 48.1 all-gather.9
  120.0 63.9 all-gather.5
  189.8 42.9 reduce-scatter.2
  416.3 101.2 reduce-scatter.4
